TPU v7x, 256 devices: a whole 4x4x8 slice. The times are simulated.
256 devices in a mesh: group: 8 (over z), dev: 32 (over x, y, core).
Axes of the slice: x: 4, y: 4, z: 8, core: 2. Of those that a mesh axis runs over, the one named last changes fastest.
Arguments:
- corpus_tokens: bfloat16 [32768, 1024], P(('group', 'dev')), may hold values from -6 to 6
- norm_gain: float32 [1024], replicated, may hold values from 0.1 to 1.9
- wi_weight: bfloat16 [1024, 5248], P('dev'), may hold values from -0.1875 to 0.1875
- wo_weight: bfloat16 [2624, 1024], P('dev'), may hold values from -0.125 to 0.125
- final_gain: float32 [1024], replicated, may hold values from 0.1 to 1.9
- proj_weight: bfloat16 [1024, 128], replicated, may hold values from -0.1875 to 0.1875
- query_vectors: bfloat16 [512, 32, 128], P(('group', 'dev')), may hold values from -6 to 6
- doc_lengths: int32 [8, 16], P('group'), may hold values from 1 to 2048, 4096 in all within a row
- candidates: int32 [512, 100], P(('group', 'dev')), may hold values from 0 to 127
Outputs:
- doc_vectors: bfloat16 [32768, 128], P(('group', 'dev'))
- scores: float32 [512, 100], P(('group', 'dev'))
Inputs may be any that keep to these rules, and one draw needn't show every extreme that they name: `doc_lengths`: each row sums to 4096; its largest length is exactly 2048. `candidates`: document k of group g has id g * 16 + k; ids may repeat within a row.
All inputs are finite; a program needn't handle non-finite values.
Results may differ from a plain program's by a relative error of at most 0.0062.
Values may be sent and summed in bfloat16 or wider, within the bound.
A program may use at most 128 MiB of HBM per device.

v0:
```python
import jax
import jax.numpy as jnp
from jax import lax
from jax.experimental import pallas as pl
from jax.experimental.pallas import tpu as pltpu
from jax.sharding import PartitionSpec as P

BLOCK = 256


def layer_norm(values, gain_row):
    values = values.astype(jnp.float32)
    center = jnp.mean(values, axis=-1, keepdims=True)
    spread = jnp.mean(jnp.square(values - center), axis=-1, keepdims=True)
    return (values - center) * lax.rsqrt(spread + 1e-05) * gain_row


def segment_maxima(ends_ref, vec_ref, query_rows, doc_count):
    tokens = vec_ref.shape[0]
    blocks = tokens // BLOCK
    width = query_rows.shape[0]
    row_ids = lax.broadcasted_iota(jnp.int32, (BLOCK, width), 0)
    doc_ids = lax.broadcasted_iota(jnp.int32, (doc_count, width), 0)

    def step(_, state):
        place, doc, best = state
        block = jnp.minimum(place // BLOCK, blocks - 1)
        first = pl.multiple_of(block * BLOCK, BLOCK)
        doc_end = ends_ref[doc]
        stop = jnp.minimum(doc_end, first + BLOCK)
        similar = lax.dot_general(
            vec_ref[pl.ds(first, BLOCK), :],
            query_rows,
            (((1,), (1,)), ((), ())),
            preferred_element_type=jnp.float32,
        )
        inside = (row_ids >= place - first) & (row_ids < stop - first)
        top = jnp.max(jnp.where(inside, similar, -jnp.inf), axis=0, keepdims=True)
        best = jnp.where(doc_ids == doc, jnp.maximum(best, top), best)
        doc = jnp.minimum(doc + (stop == doc_end).astype(jnp.int32), doc_count - 1)
        return stop, doc, best

    start = jnp.full((doc_count, width), -jnp.inf, jnp.float32)
    state = (jnp.int32(0), jnp.int32(0), start)
    return lax.fori_loop(0, blocks + doc_count - 1, step, state)[2]


def score_kernel(query_len, ends_ref, vec_ref, query_ref, out_ref):
    doc_count = out_ref.shape[0]
    best = segment_maxima(ends_ref, vec_ref, query_ref[...], doc_count).astype(jnp.bfloat16)
    rows = lax.broadcasted_iota(jnp.int32, (best.shape[1], out_ref.shape[1]), 0)
    cols = lax.broadcasted_iota(jnp.int32, (best.shape[1], out_ref.shape[1]), 1)
    adder = (rows // query_len == cols).astype(jnp.bfloat16)
    out_ref[...] = jnp.dot(best, adder, preferred_element_type=jnp.float32) / query_len


def body(
    corpus_tokens,
    norm_gain,
    wi_weight,
    wo_weight,
    final_gain,
    proj_weight,
    query_vectors,
    doc_lengths,
    candidates,
):
    groups = lax.axis_size("group")
    doc_count = doc_lengths.shape[1]
    per_query, query_len, vector_dim = query_vectors.shape
    near_queries = lax.all_gather(query_vectors, "group", axis=0, tiled=True)
    normed = layer_norm(corpus_tokens, norm_gain).astype(jnp.bfloat16)
    lifted = jnp.dot(
        normed,
        lax.all_gather(wi_weight, "dev", axis=0, tiled=True),
        preferred_element_type=jnp.float32,
    )
    hidden_width = wi_weight.shape[1] // 2
    hidden = (
        jax.nn.gelu(lifted[:, :hidden_width], approximate=False) * lifted[:, hidden_width:]
    ).astype(jnp.bfloat16)
    down_sum = jnp.dot(
        hidden,
        lax.all_gather(wo_weight, "dev", axis=0, tiled=True),
        preferred_element_type=jnp.float32,
    )
    mixed_sum = corpus_tokens.astype(jnp.float32) + down_sum
    normed_out = layer_norm(mixed_sum, final_gain).astype(jnp.bfloat16)
    projected = jnp.dot(normed_out, proj_weight, preferred_element_type=jnp.float32)
    inverse = lax.rsqrt(jnp.sum(projected * projected, axis=-1, keepdims=True) + 1e-06)
    vectors = (projected * inverse).astype(jnp.bfloat16)

    group_vectors = lax.all_gather(vectors, "dev", axis=0, tiled=True)
    doc_ends = jnp.cumsum(doc_lengths[0])
    table = pl.pallas_call(
        lambda *refs: score_kernel(query_len, *refs),
        out_shape=jax.ShapeDtypeStruct((doc_count, 128), jnp.float32),
        in_specs=[
            pl.BlockSpec(memory_space=pltpu.SMEM),
            pl.BlockSpec(memory_space=pltpu.VMEM),
            pl.BlockSpec(memory_space=pltpu.VMEM),
        ],
        out_specs=pl.BlockSpec(memory_space=pltpu.VMEM),
        name="score",
    )(doc_ends, group_vectors, near_queries.reshape(-1, vector_dim))
    totals = table[:, : groups * per_query].reshape(doc_count, groups, per_query)
    outgoing = jnp.transpose(totals, (1, 2, 0))
    incoming = lax.all_to_all(outgoing, "group", split_axis=0, concat_axis=0, tiled=True)
    score_table = jnp.transpose(incoming, (1, 0, 2)).reshape(per_query, groups * doc_count)
    labels = jnp.arange(groups * doc_count, dtype=jnp.int32)
    picked = (candidates[:, :, None] == labels[None, None, :]).astype(jnp.float32)
    scores = jnp.sum(picked * score_table[:, None, :], axis=-1)
    return (vectors, scores)


def solution(mesh):
    placed = (
        P(("group", "dev"), None),
        P(),
        P("dev", None),
        P("dev", None),
        P(),
        P(),
        P(("group", "dev"), None, None),
        P("group", None),
        P(("group", "dev"), None),
    )
    return jax.shard_map(
        body,
        mesh=mesh,
        in_specs=placed,
        out_specs=(P(("group", "dev"), None), P(("group", "dev"), None)),
        check_vma=False,
    )
```

profile of v0, /device:TPU:1, one launch (start us, length us, event | category | flops | bytes accessed | tf_op | source)
XLA Modules:
  0.0 223.9 jit_solution(5843114580571039702)
XLA Ops:
  7.2 0.0 copy-start
  7.2 0.0 all-gather.9.cloned.1.call-start
  7.2 0.7 all-gather.9.cloned.1.call-update
  7.9 0.0 all-gather.5.cloned.1.call-start
  8.0 0.7 all-gather.5.cloned.1.call-update
  8.7 0.0 all-gather.7.cloned.1.call-start
  8.7 1.1 convert_reduce_fusion
  9.8 1.2 fusion.44
  11.0 0.0 copy-start.2
  11.0 0.0 copy-start.3
  11.0 57.1 %all-gather.9.cloned.1.call-done = bf16[32,82,1024]{2,1,0:T(8,128)(2,1)} async-done(((bf16[1,82,1024]{2,1,0:T(8,128)(2,1)}), bf16[32,82,1024]{2,1,0:T(8,128)(2,1)}) %all-gather.9.cloned.1.call-update) | async-done | bytes 5373968 | tf_op jit(solution)/shard_map/all_gather | solution.py:84
  68.1 7.9 %reshape.76 = bf16[2624,1024]{1,0:T(8,128)(2,1)} reshape(bf16[32,82,1024]{2,1,0:T(8,128)(2,1)} %all-gather.9.cloned.1.call-done) | data formatting | bytes 10747904
  75.9 57.4 %all-gather.5.cloned.1.call-done = bf16[1024,5248]{1,0:T(8,128)(2,1)} async-done(((bf16[32,5248]{1,0:T(8,128)(2,1)}), bf16[1024,5248]{1,0:T(8,128)(2,1)}) %all-gather.5.cloned.1.call-update) | async-done | bytes 10747920 | tf_op jit(solution)/shard_map/all_gather | solution.py:75
  133.3 0.0 copy-done.2
  133.3 0.0 copy-done.3
  133.3 0.0 copy-start.1
  133.3 5.9 %fusion.48 = f32[128,5248]{1,0:T(8,128)S(1)} fusion(bf16[1024,5248]{1,0:T(8,128)(2,1)} %all-gather.5.cloned.1.call-done, bf16[128,1024]{1,0:T(8,128)(2,1)S(1)} %copy-done.2, f32[1024]{0:T(1024)S(1)} %copy-done.3, f32[128]{0:T(128)S(1)} %add_rsqrt_fusion.2, f32[128]{0:T(128)S(1)} %broadcast_multiply_fusion.1), kind=kOutput, calls=%fused_computation.61 | convolution fusion | flops 1376387072 | bytes 13702144 | tf_op jit(solution)/shard_map/dot_general | solution.py:73
  139.2 0.0 copy-done.1
  139.2 0.0 copy-start.5
  139.2 3.8 %fusion.87 = (f32[128]{0:T(128)S(1)}, f32[128,1024]{1,0:T(8,128)S(1)}) fusion(bf16[2624,1024]{1,0:T(8,128)(2,1)S(1)} %copy-done.1, f32[128,5248]{1,0:T(8,128)S(1)} %fusion.48, bf16[128,1024]{1,0:T(8,128)(2,1)S(1)} %copy-done.2), kind=kOutput, calls=%fused_computation.107 | convolution fusion | flops 710426496 | bytes 8913408 | tf_op jit(solution)/shard_map/dot_general | solution.py:82
  143.0 0.0 copy-start.7
  143.1 0.0 copy-start.4
  143.1 0.2 multiply_reduce_fusion
  143.3 0.0 copy-start.6
  143.3 0.0 copy-done
  143.3 0.0 copy-done.5
  143.3 0.3 multiply_reduce_fusion.1
  143.7 0.1 copy.21
  143.8 0.7 multiply_convert_fusion.2
  144.5 0.0 all-gather.7.cloned.1.call-update
  144.5 0.0 copy-done.7
  144.5 0.1 copy.23
  144.6 0.6 reduce.refs_0_
  145.3 0.0 copy-done.4
  145.3 22.0 %all_gather.15 = bf16[16,32,128]{2,1,0:T(8,128)(2,1)} all-gather(bf16[2,32,128]{2,1,0:T(8,128)(2,1)S(1)} %copy-done.4), channel_id=1, replica_groups=mesh['group'=8,'dev'=32] {'group'}, dimensions={0}, use_global_device_ids=true | all-gather | bytes 147456 | tf_op jit(solution)/shard_map/all_gather | solution.py:71
  167.2 24.9 %all-gather.7.cloned.1.call-done.refs_1_ = bf16[4096,128]{1,0:T(8,128)(2,1)} async-done(((bf16[128,128]{1,0:T(8,128)(2,1)}), bf16[4096,128]{1,0:T(8,128)(2,1)}) %all-gather.7.cloned.1.call-update) | async-done | bytes 1048592 | tf_op jit(solution)/shard_map/all_gather | solution.py:93
  192.1 9.6 %score.1 = f32[16,128]{1,0:T(8,128)} custom-call(s32[16]{0:T(128)} %reduce.refs_0_, bf16[4096,128]{1,0:T(8,128)(2,1)} %all-gather.7.cloned.1.call-done.refs_1_, bf16[512,128]{1,0:T(8,128)(2,1)} %bitcast.11), custom_call_target="tpu_custom_call" | custom-call | tf_op jit(solution)/shard_map/score/pallas_call | solution.py:95
  201.7 1.4 copy.24
  203.0 6.7 %all-to-all-start = ((f32[8,2,16]{2,1,0:T(2,128)}), f32[8,2,16]{2,1,0:T(2,128)S(1)}, u32[]{:S(2)}, u32[]{:S(2)}) async-start(f32[8,2,16]{2,1,0:T(2,128)} %bitcast.4), calls=%async_computation | async-start | bytes 16384 | tf_op jit(solution)/shard_map/all_to_all | solution.py:108
  209.8 0.0 copy-done.6
  209.8 0.1 copy.22
  209.9 6.5 %all-to-all-done = f32[8,2,16]{2,1,0:T(2,128)S(1)} async-done(((f32[8,2,16]{2,1,0:T(2,128)}), f32[8,2,16]{2,1,0:T(2,128)S(1)}, u32[]{:S(2)}, u32[]{:S(2)}) %all-to-all-start) | async-done | bytes 1056 | tf_op jit(solution)/shard_map/all_to_all | solution.py:108
  216.3 0.1 mul.88
  216.4 0.3 fusion.56
  216.7 0.6 copy.26
  (7 shorter events, 0.1 us)
Async XLA Ops:
  7.2 136.1 %copy-start = (bf16[1024,128]{1,0:T(8,128)(2,1)S(1)}, bf16[1024,128]{1,0:T(8,128)(2,1)}, u32[]{:S(2)}) copy-start(bf16[1024,128]{1,0:T(8,128)(2,1)} %param.14) | copy-start | bytes 786436
  7.2 60.9 %all-gather.9.cloned.1.call-start = ((), (), s32[]{:S(2)}) async-start(), calls=%async_computation.3 | async-start | bytes 5947392 | tf_op jit(solution)/shard_map/all_gather | solution.py:84
  7.9 125.4 %all-gather.5.cloned.1.call-start = ((), (), s32[]{:S(2)}) async-start(), calls=%async_computation.1 | async-start | bytes 11083776 | tf_op jit(solution)/shard_map/all_gather | solution.py:75
  8.7 183.4 %all-gather.7.cloned.1.call-start = ((), (), s32[]{:S(2)}) async-start(), calls=%async_computation.2 | async-start | bytes 1081344 | tf_op jit(solution)/shard_map/all_gather | solution.py:93
  11.0 122.4 %copy-start.2 = (bf16[128,1024]{1,0:T(8,128)(2,1)S(1)}, bf16[128,1024]{1,0:T(8,128)(2,1)}, u32[]{:S(2)}) copy-start(bf16[128,1024]{1,0:T(8,128)(2,1)} %param.9) | copy-start | bytes 786436
  11.0 122.4 %copy-start.3 = (f32[1024]{0:T(1024)S(1)}, f32[1024]{0:T(1024)}, u32[]{:S(2)}) copy-start(f32[1024]{0:T(1024)} %param.10) | copy-start | bytes 12292
  133.3 5.9 %copy-start.1 = (bf16[2624,1024]{1,0:T(8,128)(2,1)S(1)}, bf16[2624,1024]{1,0:T(8,128)(2,1)}, u32[]{:S(2)}) copy-start(bf16[2624,1024]{1,0:T(8,128)(2,1)} %reshape.76) | copy-start | bytes 16121860
  139.2 4.1 %copy-start.5 = (f32[1024]{0:T(1024)S(1)}, f32[1024]{0:T(1024)}, u32[]{:S(2)}) copy-start(f32[1024]{0:T(1024)} %param.13) | copy-start | bytes 12292
  143.0 1.5 copy-start.7
  143.1 2.2 copy-start.4
  143.3 66.5 %copy-start.6 = (s32[2,100]{1,0:T(2,128)S(1)}, s32[2,100]{1,0:T(2,128)}, u32[]{:S(2)}) copy-start(s32[2,100]{1,0:T(2,128)} %param.17) | copy-start | bytes 2404
  203.0 13.3 %all-to-all-start = ((f32[8,2,16]{2,1,0:T(2,128)}), f32[8,2,16]{2,1,0:T(2,128)S(1)}, u32[]{:S(2)}, u32[]{:S(2)}) async-start(f32[8,2,16]{2,1,0:T(2,128)} %bitcast.4), calls=%async_computation | async-start | bytes 16384 | tf_op jit(solution)/shard_map/all_to_all | solution.py:108
Sparse Core Ops, SparseCore 0:
  10.6 57.4 all-gather.8
  70.6 62.6 all-gather.4
  144.6 47.4 all-gather.6
where the time goes:
time: 224 us
  waiting for transfers between devices  147 us (66%)
  blocking collectives  22 us (10%)
  between operations  13.9 us (6%)
  local copies, waits for them, and re-layouts  10.3 us (5%)
  matrix products  10 us (4%)
  Pallas kernels  9.56 us (4%)
  starting transfers between devices  6.85 us (3%)
  other arithmetic  4.14 us (2%)
    all_gather x1, waiting for transfers between devices, body(): lax.all_gather(wi_weight, 'dev', axis=0, tiled=True)  57.4 us
    all_gather x1, waiting for transfers between devices, body(): lax.all_gather(wo_weight, 'dev', axis=0, tiled=True)  57.1 us
    all_gather x1, waiting for transfers between devices, body(): group_vectors = lax.all_gather(vectors, 'dev', axis=0, tiled=True)  24.9 us
    all_gather x1, blocking collectives, body(): near_queries = lax.all_gather(query_vectors, 'group', axis=0, tiled=True)  22 us
    pallas_call x1, Pallas kernels, body(): pl.pallas_call(lambda *refs: score_kernel(query_len, *refs), out_shape=ja...  9.56 us
    unnamed x19, local copies, waits for them, and re-layouts  8.66 us
    all_to_all x1, starting transfers between devices, body(): lax.all_to_all(outgoing, 'group', split_axis=0, concat_axis=0, tiled=True)  6.73 us
    all_to_all x1, waiting for transfers between devices, body(): lax.all_to_all(outgoing, 'group', split_axis=0, concat_axis=0, tiled=True)  6.45 us
  transfers between devices with their start and end apart: 4, of which 4 were waited for; matrix products, arithmetic and copies ran while one was open for 5% of the time, Pallas kernels for 0%

commit v1 on v0

--- a/solution.py
+++ b/solution.py
@@ -54,6 +54,300 @@
     out_ref[...] = jnp.dot(best, adder, preferred_element_type=jnp.float32) / query_len
 
 
+MESH = pl.DeviceIdType.MESH
+SIDE = 4
+OFFSETS = (0, -1, 1, 2)
+
+
+def place():
+    dev = lax.axis_index("dev")
+    core = dev % 2
+    chip = dev // 2
+    x, y = chip // SIDE, chip % SIDE
+
+    def at(dx, dy):
+        return (((x + dx + SIDE) % SIDE) * SIDE + (y + dy + SIDE) % SIDE) * 2 + core
+
+    return dev, dev + 1 - 2 * core, 1 - 2 * core, at
+
+
+def greet(targets):
+    barrier = pltpu.get_barrier_semaphore()
+    for target in targets:
+        pl.semaphore_signal(barrier, inc=1, device_id=target, device_id_type=MESH)
+    pl.semaphore_wait(barrier, len(targets))
+
+
+def remote(src, dst, send_sem, recv_sem, target):
+    return pltpu.make_async_remote_copy(
+        src_ref=src,
+        dst_ref=dst,
+        send_sem=send_sem,
+        recv_sem=recv_sem,
+        device_id=target,
+        device_id_type=MESH,
+    )
+
+
+def weights_kernel(
+    groups, wi, wo, query, wi_out, wo_out, query_out,
+    ring_send, ring_recv, pair_send, pair_recv, query_send, query_recv, own_sem,
+):
+    dev, partner, flip, at = place()
+    group = lax.axis_index("group")
+    depth, width = wi.shape
+    half_depth = depth // 2
+    cut = (width // 256) * 128 + 128
+    model = wo.shape[1]
+    rows = query.shape[0]
+    sent = []
+
+    def loc(p, first, second):
+        return at(first, second) if p == 0 else at(second, first)
+
+    def views(origin, p, half):
+        wi_cols = {None: (0, width), 0: (0, cut), 1: (cut, width - cut)}[half]
+        wo_cols = (p * model // 2 + (model // 4 if half == 1 else 0), model // (2 if half is None else 4))
+        if origin is None:
+            return (
+                wi.at[pl.ds(p * half_depth, half_depth), pl.ds(*wi_cols)],
+                wo.at[:, pl.ds(*wo_cols)],
+            )
+        first = pl.multiple_of(origin * depth + p * half_depth, half_depth)
+        return (
+            wi_out.at[pl.ds(first, half_depth), pl.ds(*wi_cols)],
+            wo_out.at[origin, :, pl.ds(*wo_cols)],
+        )
+
+    def copies(source, origin, p, half, sems_send, sems_recv, index, target):
+        pairs = zip(views(source, p, half), views(origin, p, half))
+        return [
+            remote(src, dst, sems_send.at[index, i], sems_recv.at[index, i], {"dev": target})
+            for i, (src, dst) in enumerate(pairs)
+        ]
+
+    def ring_index(p, slot, kind):
+        return (p * 5 + slot) * 4 + kind
+
+    def start(*args):
+        for copy in copies(*args):
+            copy.start()
+            sent.append(copy)
+
+    def ring_start(p, slot, source, origin):
+        for kind, step in ((0, 1), (1, -1)):
+            target = loc(p, step, 0) if slot == 0 else loc(p, 0, step)
+            start(source, origin, p, None, ring_send, ring_recv, ring_index(p, slot, kind), target)
+
+    def ring_pass(p, slot, kind, origin):
+        step = 1 if kind == 0 else -1
+        target = loc(p, step, 0) if slot == 0 else loc(p, 0, step)
+        start(origin, origin, p, kind, ring_send, ring_recv, ring_index(p, slot, kind + 2), target)
+
+    def ring_wait(p, slot, kind, origin):
+        half = kind - 2 if kind >= 2 else None
+        for copy in copies(origin, origin, p, half, ring_send, ring_recv, ring_index(p, slot, kind), partner):
+            copy.wait_recv()
+
+    def pair_index(p, first, second):
+        return (p * 4 + OFFSETS.index(first)) * 4 + OFFSETS.index(second)
+
+    def pair_start(p, first, second, source, origin):
+        start(source, origin, p, None, pair_send, pair_recv, pair_index(p, first, second), partner)
+
+    others = [(group + k) % groups for k in range(1, groups)]
+    greet(
+        [{"dev": at(*d)} for d in ((1, 0), (-1, 0), (0, 1), (0, -1))]
+        + [{"dev": partner}]
+        + [{"group": other} for other in others]
+    )
+    for p in (0, 1):
+        ring_start(p, 0, None, dev)
+    for p in (0, 1):
+        ring_start(p, 1, None, dev)
+        pair_start(p, 0, 0, None, dev)
+    own_rows = pl.ds(pl.multiple_of(group * rows, rows), rows)
+    for k, other in enumerate(others):
+        copy = remote(query, query_out.at[own_rows], query_send.at[k], query_recv.at[k], {"group": other})
+        copy.start()
+        sent.append(copy)
+    kept = [
+        pltpu.make_async_copy(wi, wi_out.at[pl.ds(pl.multiple_of(dev * depth, depth), depth)], own_sem.at[0]),
+        pltpu.make_async_copy(wo, wo_out.at[dev], own_sem.at[1]),
+        pltpu.make_async_copy(query, query_out.at[own_rows], own_sem.at[2]),
+    ]
+    for copy in kept:
+        copy.start()
+
+    for slot, first, kind in ((2, -1, 0), (3, 1, 1)):
+        for p in (0, 1):
+            origin = loc(p, first, 0)
+            ring_wait(p, 0, kind, origin)
+            ring_pass(p, 0, kind, origin)
+            ring_start(p, slot, origin, origin)
+            pair_start(p, first, 0, origin, origin)
+    for p in (0, 1):
+        origin = loc(p, 2, 0)
+        ring_wait(p, 0, 2, origin)
+        ring_wait(p, 0, 3, origin)
+        ring_start(p, 4, origin, origin)
+        pair_start(p, 2, 0, origin, origin)
+    for slot, first in ((1, 0), (2, -1), (3, 1), (4, 2)):
+        for second, kind in ((-1, 0), (1, 1)):
+            for p in (0, 1):
+                origin = loc(p, first, second)
+                ring_wait(p, slot, kind, origin)
+                ring_pass(p, slot, kind, origin)
+                pair_start(p, first, second, origin, origin)
+    for slot, first in ((1, 0), (2, -1), (3, 1), (4, 2)):
+        for p in (0, 1):
+            origin = loc(p, first, 2)
+            ring_wait(p, slot, 2, origin)
+            ring_wait(p, slot, 3, origin)
+            pair_start(p, first, 2, origin, origin)
+
+    for k in range(groups - 1):
+        source = (group + groups - 1 - k) % groups
+        landing = query_out.at[pl.ds(pl.multiple_of(source * rows, rows), rows)]
+        remote(query, landing, query_send.at[k], query_recv.at[k], {"dev": partner}).wait_recv()
+    for first in OFFSETS:
+        for second in OFFSETS:
+            for p in (0, 1):
+                origin = loc(p, first, second) + flip
+                index = pair_index(p, first, second)
+                for copy in copies(origin, origin, p, None, pair_send, pair_recv, index, partner):
+                    copy.wait_recv()
+    for copy in sent:
+        copy.wait_send()
+    for copy in kept:
+        copy.wait()
+
+
+def gather_weights(wi_weight, wo_weight, query_rows, groups, devs):
+    depth, width = wi_weight.shape
+    kept_rows, model = wo_weight.shape
+    rows, vector_dim = query_rows.shape
+    return pl.pallas_call(
+        lambda *refs: weights_kernel(groups, *refs),
+        out_shape=(
+            jax.ShapeDtypeStruct((devs * depth, width), wi_weight.dtype),
+            jax.ShapeDtypeStruct((devs, kept_rows, model), wo_weight.dtype),
+            jax.ShapeDtypeStruct((groups * rows, vector_dim), query_rows.dtype),
+        ),
+        in_specs=[pl.BlockSpec(memory_space=pltpu.VMEM)] * 3,
+        out_specs=[pl.BlockSpec(memory_space=pl.ANY)] * 3,
+        scratch_shapes=[
+            pltpu.SemaphoreType.DMA((40, 2)),
+            pltpu.SemaphoreType.DMA((40, 2)),
+            pltpu.SemaphoreType.DMA((32, 2)),
+            pltpu.SemaphoreType.DMA((32, 2)),
+            pltpu.SemaphoreType.DMA((groups - 1,)),
+            pltpu.SemaphoreType.DMA((groups - 1,)),
+            pltpu.SemaphoreType.DMA((3,)),
+        ],
+        compiler_params=pltpu.CompilerParams(collective_id=0, has_side_effects=True),
+        name="weights",
+    )(wi_weight, wo_weight, query_rows)
+
+
+def vectors_kernel(vec, out, send_sem, recv_sem, pair_send, pair_recv, own_sem):
+    dev, partner, flip, at = place()
+    rows = vec.shape[0]
+
+    def block(origin):
+        return out.at[pl.ds(pl.multiple_of(origin * rows, rows), rows)]
+
+    steps = [(dx, dy) for dx in OFFSETS for dy in OFFSETS if (dx, dy) != (0, 0)]
+    steps.sort(key=lambda d: -abs(d[0]) - abs(d[1]))
+    greet([{"dev": at(dx, dy)} for dx, dy in steps] + [{"dev": partner}])
+    sent = []
+    for k, (dx, dy) in enumerate(steps):
+        sent.append(remote(vec, block(dev), send_sem.at[k], recv_sem.at[k], {"dev": at(dx, dy)}))
+        sent[-1].start()
+    sent.append(remote(vec, block(dev), pair_send.at[15], pair_recv.at[15], {"dev": partner}))
+    sent[-1].start()
+    kept = pltpu.make_async_copy(vec, block(dev), own_sem)
+    kept.start()
+    for k, (dx, dy) in reversed(list(enumerate(steps))):
+        origin = at(-dx, -dy)
+        remote(vec, block(origin), send_sem.at[k], recv_sem.at[k], {"dev": partner}).wait_recv()
+        sent.append(remote(block(origin), block(origin), pair_send.at[k], pair_recv.at[k], {"dev": partner}))
+        sent[-1].start()
+    for k, (dx, dy) in enumerate(steps + [(0, 0)]):
+        origin = at(-dx, -dy) + flip
+        remote(vec, block(origin), pair_send.at[k], pair_recv.at[k], {"dev": partner}).wait_recv()
+    for copy in sent:
+        copy.wait_send()
+    kept.wait()
+
+
+def gather_vectors(vectors, devs):
+    rows, vector_dim = vectors.shape
+    return pl.pallas_call(
+        vectors_kernel,
+        out_shape=jax.ShapeDtypeStruct((devs * rows, vector_dim), vectors.dtype),
+        in_specs=[pl.BlockSpec(memory_space=pltpu.VMEM)],
+        out_specs=pl.BlockSpec(memory_space=pltpu.VMEM),
+        scratch_shapes=[
+            pltpu.SemaphoreType.DMA((15,)),
+            pltpu.SemaphoreType.DMA((15,)),
+            pltpu.SemaphoreType.DMA((16,)),
+            pltpu.SemaphoreType.DMA((16,)),
+            pltpu.SemaphoreType.DMA,
+        ],
+        compiler_params=pltpu.CompilerParams(collective_id=1, has_side_effects=True),
+        name="vectors",
+    )(vectors)
+
+
+def pick_kernel(groups, table, wanted, out, tables, send_sem, recv_sem, own_sem):
+    group = lax.axis_index("group")
+    others = [(group + k) % groups for k in range(1, groups)]
+    greet([{"group": other} for other in others])
+    sent = []
+    for k, other in enumerate(others):
+        sent.append(remote(table, tables.at[group], send_sem.at[k], recv_sem.at[k], {"group": other}))
+        sent[-1].start()
+    kept = pltpu.make_async_copy(table, tables.at[group], own_sem)
+    kept.start()
+    per_query, listed = wanted.shape
+    docs = table.shape[0]
+    for k in range(groups - 1):
+        source = (group + groups - 1 - k) % groups
+        remote(table, tables.at[source], send_sem.at[k], recv_sem.at[k], {"group": other}).wait_recv()
+    kept.wait()
+    for copy in sent:
+        copy.wait_send()
+    lanes = lax.broadcasted_iota(jnp.int32, (docs, table.shape[1]), 1)
+    labels = lax.broadcasted_iota(jnp.int32, (docs, listed), 0)
+    for q in range(per_query):
+        row = wanted[pl.ds(q, 1), :]
+        total = jnp.zeros((1, listed), jnp.float32)
+        for g in range(groups):
+            mine = jnp.where(lanes == group * per_query + q, tables[g], 0.0)
+            column = jnp.sum(mine, axis=1, keepdims=True)
+            hit = jnp.where(labels + g * docs == row, column, 0.0)
+            total = total + jnp.sum(hit, axis=0, keepdims=True)
+        out[pl.ds(q, 1), :] = total
+
+
+def pick_scores(table, candidates, groups):
+    return pl.pallas_call(
+        lambda *refs: pick_kernel(groups, *refs),
+        out_shape=jax.ShapeDtypeStruct(candidates.shape, jnp.float32),
+        in_specs=[pl.BlockSpec(memory_space=pltpu.VMEM)] * 2,
+        out_specs=pl.BlockSpec(memory_space=pltpu.VMEM),
+        scratch_shapes=[
+            pltpu.VMEM((groups,) + table.shape, jnp.float32),
+            pltpu.SemaphoreType.DMA((groups - 1,)),
+            pltpu.SemaphoreType.DMA((groups - 1,)),
+            pltpu.SemaphoreType.DMA,
+        ],
+        compiler_params=pltpu.CompilerParams(collective_id=2, has_side_effects=True),
+        name="pick",
+    )(table, candidates)
+
+
 def body(
     corpus_tokens,
     norm_gain,
@@ -68,11 +362,14 @@
     groups = lax.axis_size("group")
     doc_count = doc_lengths.shape[1]
     per_query, query_len, vector_dim = query_vectors.shape
-    near_queries = lax.all_gather(query_vectors, "group", axis=0, tiled=True)
+    devs = lax.axis_size("dev")
+    wi_full, wo_blocks, near_queries = gather_weights(
+        wi_weight, wo_weight, query_vectors.reshape(-1, vector_dim), groups, devs
+    )
     normed = layer_norm(corpus_tokens, norm_gain).astype(jnp.bfloat16)
     lifted = jnp.dot(
         normed,
-        lax.all_gather(wi_weight, "dev", axis=0, tiled=True),
+        wi_full,
         preferred_element_type=jnp.float32,
     )
     hidden_width = wi_weight.shape[1] // 2
@@ -81,7 +378,7 @@
     ).astype(jnp.bfloat16)
     down_sum = jnp.dot(
         hidden,
-        lax.all_gather(wo_weight, "dev", axis=0, tiled=True),
+        wo_blocks.reshape(hidden_width, -1),
         preferred_element_type=jnp.float32,
     )
     mixed_sum = corpus_tokens.astype(jnp.float32) + down_sum
@@ -90,7 +387,7 @@
     inverse = lax.rsqrt(jnp.sum(projected * projected, axis=-1, keepdims=True) + 1e-06)
     vectors = (projected * inverse).astype(jnp.bfloat16)
 
-    group_vectors = lax.all_gather(vectors, "dev", axis=0, tiled=True)
+    group_vectors = gather_vectors(vectors, devs)
     doc_ends = jnp.cumsum(doc_lengths[0])
     table = pl.pallas_call(
         lambda *refs: score_kernel(query_len, *refs),
@@ -102,14 +399,8 @@
         ],
         out_specs=pl.BlockSpec(memory_space=pltpu.VMEM),
         name="score",
-    )(doc_ends, group_vectors, near_queries.reshape(-1, vector_dim))
-    totals = table[:, : groups * per_query].reshape(doc_count, groups, per_query)
-    outgoing = jnp.transpose(totals, (1, 2, 0))
-    incoming = lax.all_to_all(outgoing, "group", split_axis=0, concat_axis=0, tiled=True)
-    score_table = jnp.transpose(incoming, (1, 0, 2)).reshape(per_query, groups * doc_count)
-    labels = jnp.arange(groups * doc_count, dtype=jnp.int32)
-    picked = (candidates[:, :, None] == labels[None, None, :]).astype(jnp.float32)
-    scores = jnp.sum(picked * score_table[:, None, :], axis=-1)
+    )(doc_ends, group_vectors, near_queries)
+    scores = pick_scores(table, candidates, groups)
     return (vectors, scores)
 
 

time: 224 us -> 122 us (0.54)
  waiting for transfers between devices: 147 us -> 0 us
  Pallas kernels: 9.56 us -> 95 us
  blocking collectives: 22 us -> 0 us
  between operations: 13.9 us -> 0.74 us
  starting transfers between devices: 6.85 us -> 0 us
  matrix products: 10 us -> 12.5 us
    all_gather x3 -> x0, waiting for transfers between devices: 139 us -> none  [the longest x1 57.4 us: body(): lax.all_gather(wi_weight, 'dev', axis=0, tiled=True)]
    pallas_call x0 -> x3, Pallas kernels: none -> 85.5 us  [the longest x1 60.8 us: gather_weights(): pl.pallas_call(lambda *refs: weights_kernel(groups, *refs), out_shape=(ja...]
    all_gather x1 -> x0, blocking collectives: 22 us -> none  [body(): near_queries = lax.all_gather(query_vectors, 'group', axis=0, tiled=True)]
    reshape x0 -> x1, local copies, waits for them, and re-layouts: none -> 7.88 us  [body(): wo_blocks.reshape(hidden_width, -1)]
    unnamed x19 -> x9, local copies, waits for them, and re-layouts: 8.66 us -> 1.27 us
    all_to_all x1 -> x0, starting transfers between devices: 6.73 us -> none  [body(): lax.all_to_all(outgoing, 'group', split_axis=0, concat_axis=0, tiled=True)]
    all_to_all x1 -> x0, waiting for transfers between devices: 6.45 us -> none  [body(): lax.all_to_all(outgoing, 'group', split_axis=0, concat_axis=0, tiled=True)]
    dot_general x2, matrix products: 9.67 us -> 12.2 us  [the longest x1 6.35 us: body(): jnp.dot(hidden, wo_blocks.reshape(hidden_width, -1), preferred_element_ty...]
  transfers between devices with their start and end apart: 4 -> 0, of which waited for: 4 -> 0; matrix products, arithmetic and copies ran while one was open for 5% -> 0% of each run, Pallas kernels for 0% -> 0%
where the time goes in v1:
time: 122 us; the launch traced here: 121 us
  Pallas kernels  95 us (78%)
  matrix products  12.5 us (10%)
  local copies, waits for them, and re-layouts  9.33 us (8%)
  other arithmetic  3.84 us (3%)
    pallas_call x1, Pallas kernels, gather_weights(): pl.pallas_call(lambda *refs: weights_kernel(groups, *refs), out_shape=(ja...  60.8 us
    pallas_call x1, Pallas kernels, gather_vectors(): pl.pallas_call(vectors_kernel, out_shape=jax.ShapeDtypeStruct((devs * row...  16 us
    pallas_call x1, Pallas kernels, body(): pl.pallas_call(lambda *refs: score_kernel(query_len, *refs), out_shape=ja...  9.56 us
    pallas_call x1, Pallas kernels, pick_scores(): pl.pallas_call(lambda *refs: pick_kernel(groups, *refs), out_shape=jax.Sh...  8.62 us
    reshape x1, local copies, waits for them, and re-layouts, body(): wo_blocks.reshape(hidden_width, -1)  7.88 us
    dot_general x1, matrix products, body(): jnp.dot(hidden, wo_blocks.reshape(hidden_width, -1), preferred_element_ty...  6.35 us
    dot_general x1, matrix products, body(): lifted = jnp.dot(normed, wi_full, preferred_element_type=jnp.float32)  5.84 us

profile of v1, /device:TPU:1, one launch (start us, length us, event | category | flops | bytes accessed | tf_op | source)
XLA Modules:
  0.0 121.4 jit_solution(2895930014045226853)
XLA Ops:
  0.6 0.0 copy-start
  0.6 60.8 %weights.1 = (bf16[1024,5248]{1,0:T(8,128)(2,1)}, bf16[32,82,1024]{2,1,0:T(8,128)(2,1)}, bf16[512,128]{1,0:T(8,128)(2,1)}) custom-call(bf16[32,5248]{1,0:T(8,128)(2,1)} %refs_0_.1, bf16[82,1024]{1,0:T(8,128)(2,1)} %refs_1_.2, bf16[64,128]{1,0:T(8,128)(2,1)} %bitcast.5), custom_call_target="tpu_custom_call" | custom-call | tf_op jit(solution)/shard_map/weights/pallas_call | solution.py:230
  61.5 1.1 convert_reduce_fusion
  62.6 1.2 fusion.44
  63.7 5.8 %fusion.48 = f32[128,5248]{1,0:T(8,128)S(1)} fusion(bf16[1024,5248]{1,0:T(8,128)(2,1)} %get-tuple-element.5, bf16[128,1024]{1,0:T(8,128)(2,1)} %param.9, f32[1024]{0:T(1024)} %param.10, f32[128]{0:T(128)S(1)} %add_rsqrt_fusion.2, f32[128]{0:T(128)S(1)} %broadcast_multiply_fusion.1), kind=kOutput, calls=%fused_computation.61 | convolution fusion | flops 1376387072 | bytes 13702144 | tf_op jit(solution)/shard_map/dot_general | solution.py:370
  69.6 0.0 copy-start.1
  69.6 7.9 %reshape.70 = bf16[2624,1024]{1,0:T(8,128)(2,1)} reshape(bf16[32,82,1024]{2,1,0:T(8,128)(2,1)} %get-tuple-element.6) | data formatting | bytes 10747904 | tf_op jit(solution)/shard_map/reshape | solution.py:381
  77.5 0.0 copy-done.1
  77.5 0.0 copy-start.2
  77.5 6.3 %fusion.86 = (f32[128]{0:T(128)S(1)}, f32[128,1024]{1,0:T(8,128)S(1)}) fusion(bf16[2624,1024]{1,0:T(8,128)(2,1)} %reshape.70, f32[128,5248]{1,0:T(8,128)S(1)} %fusion.48, bf16[128,1024]{1,0:T(8,128)(2,1)S(1)} %copy-done.1), kind=kOutput, calls=%fused_computation.105 | convolution fusion | flops 710426496 | bytes 8913408 | tf_op jit(solution)/shard_map/dot_general | solution.py:379
  83.8 0.0 copy-start.3
  83.9 0.2 multiply_reduce_fusion
  84.1 0.0 copy-done
  84.1 0.0 copy-done.2
  84.1 0.3 multiply_reduce_fusion.1
  84.4 0.1 copy.13
  84.5 0.7 multiply_convert_fusion.2.vec
  85.2 16.0 %vectors.1.refs_1_ = bf16[4096,128]{1,0:T(8,128)(2,1)} custom-call(bf16[128,128]{1,0:T(8,128)(2,1)} %multiply_convert_fusion.2.vec), custom_call_target="tpu_custom_call" | custom-call | tf_op jit(solution)/shard_map/vectors/pallas_call | solution.py:286
  101.3 0.0 copy-done.3
  101.3 0.1 copy.14
  101.4 0.6 reduce.refs_0_
  102.0 9.6 %score.1.refs_0_ = f32[16,128]{1,0:T(8,128)} custom-call(s32[16]{0:T(128)} %reduce.refs_0_, bf16[4096,128]{1,0:T(8,128)(2,1)} %vectors.1.refs_1_, bf16[512,128]{1,0:T(8,128)(2,1)} %get-tuple-element.7.refs_2_), custom_call_target="tpu_custom_call" | custom-call | tf_op jit(solution)/shard_map/score/pallas_call | solution.py:392
  111.6 8.6 %pick.1 = f32[2,100]{1,0:T(2,128)} custom-call(f32[16,128]{1,0:T(8,128)} %score.1.refs_0_, s32[2,100]{1,0:T(2,128)} %refs_1_.3), custom_call_target="tpu_custom_call" | custom-call | tf_op jit(solution)/shard_map/pick/pallas_call | solution.py:335
  120.2 1.2 %copy.16 = f32[2,100]{1,0:T(2,128)} copy(f32[2,100]{1,0:T(2,128)} %pick.1) | data formatting | bytes 1600
  (6 shorter events, 0.1 us)
Async XLA Ops:
  0.6 83.4 %copy-start = (bf16[1024,128]{1,0:T(8,128)(2,1)S(1)}, bf16[1024,128]{1,0:T(8,128)(2,1)}, u32[]{:S(2)}) copy-start(bf16[1024,128]{1,0:T(8,128)(2,1)} %param.14) | copy-start | bytes 786436
  69.6 7.9 %copy-start.1 = (bf16[128,1024]{1,0:T(8,128)(2,1)S(1)}, bf16[128,1024]{1,0:T(8,128)(2,1)}, u32[]{:S(2)}) copy-start(bf16[128,1024]{1,0:T(8,128)(2,1)} %param.9) | copy-start | bytes 786436
  77.5 6.6 %copy-start.2 = (f32[1024]{0:T(1024)S(1)}, f32[1024]{0:T(1024)}, u32[]{:S(2)}) copy-start(f32[1024]{0:T(1024)} %param.13) | copy-start | bytes 12292
  83.8 17.4 %copy-start.3 = (s32[1,16]{1,0:T(1,128)S(1)}, s32[1,16]{1,0:T(1,128)}, u32[]{:S(2)}) copy-start(s32[1,16]{1,0:T(1,128)} %param.16) | copy-start | bytes 196

commit v2 on v1

--- a/solution.py
+++ b/solution.py
@@ -57,6 +57,7 @@
 MESH = pl.DeviceIdType.MESH
 SIDE = 4
 OFFSETS = (0, -1, 1, 2)
+TILE = 512
 
 
 def place():
@@ -90,7 +91,8 @@
 
 
 def weights_kernel(
-    groups, wi, wo, query, wi_out, wo_out, query_out,
+    groups, wi, wo, query, tokens, norm_gain, final_gain, proj, query_out, vec_out,
+    wi_out, wo_out, normed, lifted, hidden, mixed,
     ring_send, ring_recv, pair_send, pair_recv, query_send, query_recv, own_sem,
 ):
     dev, partner, flip, at = place()
@@ -178,6 +180,7 @@
     ]
     for copy in kept:
         copy.start()
+    normed[...] = layer_norm(tokens[...], norm_gain[...]).astype(jnp.bfloat16)
 
     for slot, first, kind in ((2, -1, 0), (3, 1, 1)):
         for p in (0, 1):
@@ -217,26 +220,65 @@
                 index = pair_index(p, first, second)
                 for copy in copies(origin, origin, p, None, pair_send, pair_recv, index, partner):
                     copy.wait_recv()
+    for copy in kept:
+        copy.wait()
+
+    @pl.loop(0, width // TILE)
+    def _(j):
+        cols = pl.ds(pl.multiple_of(j * TILE, TILE), TILE)
+        lifted[:, cols] = jnp.dot(normed[...], wi_out[:, cols], preferred_element_type=jnp.float32)
+
+    if width % TILE:
+        cols = pl.ds(width - width % TILE, width % TILE)
+        lifted[:, cols] = jnp.dot(normed[...], wi_out[:, cols], preferred_element_type=jnp.float32)
+
+    @pl.loop(0, hidden.shape[0] // 16)
+    def _(i):
+        strip = pl.ds(pl.multiple_of(i * 16, 16), 16)
+        both = lifted[strip, :]
+        gated = both[:, : width // 2]
+        gelu = 0.5 * gated * (1.0 + lax.erf(gated * 0.5**0.5))
+        hidden[strip, :] = (gelu * both[:, width // 2 :]).astype(jnp.bfloat16)
+
+    mixed[...] = tokens[...].astype(jnp.float32)
+    kept_rows = wo.shape[0]
+    for k in range(0, wo_out.shape[0], 4):
+        part = None
+        for i in range(k, k + 4):
+            term = jnp.dot(
+                hidden[:, i * kept_rows : (i + 1) * kept_rows],
+                wo_out[i],
+                preferred_element_type=jnp.float32,
+            )
+            part = term if part is None else part + term
+        mixed[...] += part
+    normed_out = layer_norm(mixed[...], final_gain[...]).astype(jnp.bfloat16)
+    projected = jnp.dot(normed_out, proj[...], preferred_element_type=jnp.float32)
+    inverse = lax.rsqrt(jnp.sum(projected * projected, axis=-1, keepdims=True) + 1e-06)
+    vec_out[...] = (projected * inverse).astype(jnp.bfloat16)
     for copy in sent:
         copy.wait_send()
-    for copy in kept:
-        copy.wait()
-
-
-def gather_weights(wi_weight, wo_weight, query_rows, groups, devs):
+
+
+def encode(wi_weight, wo_weight, query_rows, tokens, norm_gain, final_gain, proj, groups, devs):
     depth, width = wi_weight.shape
     kept_rows, model = wo_weight.shape
     rows, vector_dim = query_rows.shape
     return pl.pallas_call(
         lambda *refs: weights_kernel(groups, *refs),
         out_shape=(
-            jax.ShapeDtypeStruct((devs * depth, width), wi_weight.dtype),
-            jax.ShapeDtypeStruct((devs, kept_rows, model), wo_weight.dtype),
             jax.ShapeDtypeStruct((groups * rows, vector_dim), query_rows.dtype),
+            jax.ShapeDtypeStruct((tokens.shape[0], vector_dim), jnp.bfloat16),
         ),
-        in_specs=[pl.BlockSpec(memory_space=pltpu.VMEM)] * 3,
-        out_specs=[pl.BlockSpec(memory_space=pl.ANY)] * 3,
+        in_specs=[pl.BlockSpec(memory_space=pltpu.VMEM)] * 7,
+        out_specs=[pl.BlockSpec(memory_space=pltpu.VMEM)] * 2,
         scratch_shapes=[
+            pltpu.VMEM((devs * depth, width), wi_weight.dtype),
+            pltpu.VMEM((devs, kept_rows, model), wo_weight.dtype),
+            pltpu.VMEM(tokens.shape, jnp.bfloat16),
+            pltpu.VMEM((tokens.shape[0], width), jnp.float32),
+            pltpu.VMEM((tokens.shape[0], width // 2), jnp.bfloat16),
+            pltpu.VMEM(tokens.shape, jnp.float32),
             pltpu.SemaphoreType.DMA((40, 2)),
             pltpu.SemaphoreType.DMA((40, 2)),
             pltpu.SemaphoreType.DMA((32, 2)),
@@ -246,8 +288,8 @@
             pltpu.SemaphoreType.DMA((3,)),
         ],
         compiler_params=pltpu.CompilerParams(collective_id=0, has_side_effects=True),
-        name="weights",
-    )(wi_weight, wo_weight, query_rows)
+        name="encode",
+    )(wi_weight, wo_weight, query_rows, tokens, norm_gain, final_gain, proj)
 
 
 def vectors_kernel(vec, out, send_sem, recv_sem, pair_send, pair_recv, own_sem):
@@ -363,30 +405,17 @@
     doc_count = doc_lengths.shape[1]
     per_query, query_len, vector_dim = query_vectors.shape
     devs = lax.axis_size("dev")
-    wi_full, wo_blocks, near_queries = gather_weights(
-        wi_weight, wo_weight, query_vectors.reshape(-1, vector_dim), groups, devs
+    near_queries, vectors = encode(
+        wi_weight,
+        wo_weight,
+        query_vectors.reshape(-1, vector_dim),
+        corpus_tokens,
+        norm_gain.reshape(1, -1),
+        final_gain.reshape(1, -1),
+        proj_weight,
+        groups,
+        devs,
     )
-    normed = layer_norm(corpus_tokens, norm_gain).astype(jnp.bfloat16)
-    lifted = jnp.dot(
-        normed,
-        wi_full,
-        preferred_element_type=jnp.float32,
-    )
-    hidden_width = wi_weight.shape[1] // 2
-    hidden = (
-        jax.nn.gelu(lifted[:, :hidden_width], approximate=False) * lifted[:, hidden_width:]
-    ).astype(jnp.bfloat16)
-    down_sum = jnp.dot(
-        hidden,
-        wo_blocks.reshape(hidden_width, -1),
-        preferred_element_type=jnp.float32,
-    )
-    mixed_sum = corpus_tokens.astype(jnp.float32) + down_sum
-    normed_out = layer_norm(mixed_sum, final_gain).astype(jnp.bfloat16)
-    projected = jnp.dot(normed_out, proj_weight, preferred_element_type=jnp.float32)
-    inverse = lax.rsqrt(jnp.sum(projected * projected, axis=-1, keepdims=True) + 1e-06)
-    vectors = (projected * inverse).astype(jnp.bfloat16)
-
     group_vectors = gather_vectors(vectors, devs)
     doc_ends = jnp.cumsum(doc_lengths[0])
     table = pl.pallas_call(

time: 122 us -> 105 us (0.86)
  matrix products: 12.5 us -> 0 us
  local copies, waits for them, and re-layouts: 9.33 us -> 1.97 us
  Pallas kernels: 95 us -> 101 us
  other arithmetic: 3.84 us -> 0.67 us
    dot_general x3 -> x0, matrix products: 12.5 us -> none  [the longest x1 6.35 us: body(): jnp.dot(hidden, wo_blocks.reshape(hidden_width, -1), preferred_element_ty...]
    reshape x1 -> x0, local copies, waits for them, and re-layouts: 7.88 us -> none  [body(): wo_blocks.reshape(hidden_width, -1)]
    pallas_call x1, Pallas kernels: 60.8 us -> 68 us  [encode(): pl.pallas_call(lambda *refs: weights_kernel(groups, *refs), out_shape=(ja...]
    reduce_sum x3 -> x0, other arithmetic: 2.43 us -> none  [the longest x2 1.37 us: layer_norm(): spread = jnp.mean(jnp.square(values - center), axis=-1, keepdims=True)]
where the time goes in v2:
time: 105 us
  Pallas kernels  101 us (96%)
  local copies, waits for them, and re-layouts  1.97 us (2%)
    pallas_call x1, Pallas kernels, encode(): pl.pallas_call(lambda *refs: weights_kernel(groups, *refs), out_shape=(ja...  68 us
    pallas_call x1, Pallas kernels, gather_vectors(): pl.pallas_call(vectors_kernel, out_shape=jax.ShapeDtypeStruct((devs * row...  15.1 us
    pallas_call x1, Pallas kernels, body(): pl.pallas_call(lambda *refs: score_kernel(query_len, *refs), out_shape=ja...  9.57 us
    pallas_call x1, Pallas kernels, pick_scores(): pl.pallas_call(lambda *refs: pick_kernel(groups, *refs), out_shape=jax.Sh...  8.59 us

profile of v2, /device:TPU:1, one launch (start us, length us, event | category | flops | bytes accessed | tf_op | source)
XLA Modules:
  0.0 104.6 jit_solution(14435371236077885631)
XLA Ops:
  0.6 68.0 %encode.1 = (bf16[512,128]{1,0:T(8,128)(2,1)}, bf16[128,128]{1,0:T(8,128)(2,1)}) custom-call(bf16[32,5248]{1,0:T(8,128)(2,1)} %refs_0_.1, bf16[82,1024]{1,0:T(8,128)(2,1)} %refs_1_.2, bf16[64,128]{1,0:T(8,128)(2,1)} %bitcast.4, bf16[128,1024]{1,0:T(8,128)(2,1)} %refs_3_.1, f32[1,1024]{1,0:T(1,128)} %bitcast.5, f32[1,1024]{1,0:T(1,128)} %bitcast.6, ...), custom_call_target="tpu_custom_call" | custom-call | tf_op jit(solution)/shard_map/encode/pallas_call | solution.py:267
  68.6 15.1 %vectors.1.refs_1_ = bf16[4096,128]{1,0:T(8,128)(2,1)} custom-call(bf16[128,128]{1,0:T(8,128)(2,1)} %get-tuple-element.8.vec), custom_call_target="tpu_custom_call" | custom-call | tf_op jit(solution)/shard_map/vectors/pallas_call | solution.py:328
  83.8 0.0 copy-start.2
  83.8 0.6 copy-done.2
  84.4 0.1 copy.12
  84.5 0.6 reduce.refs_0_
  85.2 0.0 copy-start
  85.2 9.6 %score.1.refs_0_ = f32[16,128]{1,0:T(8,128)} custom-call(s32[16]{0:T(128)} %reduce.refs_0_, bf16[4096,128]{1,0:T(8,128)(2,1)} %vectors.1.refs_1_, bf16[512,128]{1,0:T(8,128)(2,1)} %get-tuple-element.5.refs_2_), custom_call_target="tpu_custom_call" | custom-call | tf_op jit(solution)/shard_map/score/pallas_call | solution.py:421
  94.7 8.6 %pick.1 = f32[2,100]{1,0:T(2,128)} custom-call(f32[16,128]{1,0:T(8,128)} %score.1.refs_0_, s32[2,100]{1,0:T(2,128)} %refs_1_.3), custom_call_target="tpu_custom_call" | custom-call | tf_op jit(solution)/shard_map/pick/pallas_call | solution.py:377
  103.3 0.0 copy-done
  103.3 0.0 copy-start.1
  103.4 0.6 copy.15
  104.0 0.1 copy-done.1
  104.0 0.6 copy.16
  (1 shorter events, 0.0 us)
Async XLA Ops:
  83.8 0.7 copy-start.2
  85.2 18.2 %copy-start = (bf16[128,128]{1,0:T(8,128)(2,1)S(1)}, bf16[128,128]{1,0:T(8,128)(2,1)}, u32[]{:S(2)}) copy-start(bf16[128,128]{1,0:T(8,128)(2,1)} %get-tuple-element.8.vec) | copy-start | bytes 98308
  103.3 0.7 copy-start.1

commit v3 on v2

--- a/solution.py
+++ b/solution.py
@@ -93,13 +93,17 @@
 def weights_kernel(
     groups, wi, wo, query, tokens, norm_gain, final_gain, proj, query_out, vec_out,
     wi_out, wo_out, normed, lifted, hidden, mixed,
-    ring_send, ring_recv, pair_send, pair_recv, query_send, query_recv, own_sem,
+    ring_send, ring_recv, pair_send, pair_recv, side_send, side_recv, late_send, late_recv, query_send, query_recv, own_sem,
 ):
     dev, partner, flip, at = place()
     group = lax.axis_index("group")
     depth, width = wi.shape
     half_depth = depth // 2
-    cut = (width // 256) * 128 + 128
+    odd = group % 2
+    tiles = width // 128
+    side = (tiles // 3) * 128
+    across = (tiles - tiles // 3) * 128
+    cut = (across * 3 // 7) // 128 * 128
     model = wo.shape[1]
     rows = query.shape[0]
     sent = []
@@ -107,9 +111,30 @@
     def loc(p, first, second):
         return at(first, second) if p == 0 else at(second, first)
 
-    def views(origin, p, half):
-        wi_cols = {None: (0, width), 0: (0, cut), 1: (cut, width - cut)}[half]
-        wo_cols = (p * model // 2 + (model // 4 if half == 1 else 0), model // (2 if half is None else 4))
+    wo_side = model // 8
+    wo_across = model // 2 - wo_side
+
+    def aligned(first):
+        return pl.multiple_of(first, 128)
+
+    def views(origin, p, part):
+        wi_cols = {
+            "own": (0, width),
+            "all": (aligned(odd * side), across),
+            0: (aligned(odd * side), cut),
+            1: (aligned(odd * side + cut), across - cut),
+            "give": (aligned(odd * across), side),
+            "take": (aligned((1 - odd) * across), side),
+        }[part]
+        base = p * (model // 2)
+        wo_cols = {
+            "own": (base, model // 2),
+            "all": (aligned(base + odd * wo_side), wo_across),
+            0: (aligned(base + odd * wo_side), 2 * wo_side),
+            1: (aligned(base + odd * wo_side + 2 * wo_side), wo_across - 2 * wo_side),
+            "give": (aligned(base + odd * wo_across), wo_side),
+            "take": (aligned(base + (1 - odd) * wo_across), wo_side),
+        }[part]
         if origin is None:
             return (
                 wi.at[pl.ds(p * half_depth, half_depth), pl.ds(*wi_cols)],
@@ -124,7 +149,7 @@
     def copies(source, origin, p, half, sems_send, sems_recv, index, target):
         pairs = zip(views(source, p, half), views(origin, p, half))
         return [
-            remote(src, dst, sems_send.at[index, i], sems_recv.at[index, i], {"dev": target})
+            remote(src, dst, sems_send.at[index, i], sems_recv.at[index, i], target if isinstance(target, dict) else {"dev": target})
             for i, (src, dst) in enumerate(pairs)
         ]
 
@@ -139,7 +164,7 @@
     def ring_start(p, slot, source, origin):
         for kind, step in ((0, 1), (1, -1)):
             target = loc(p, step, 0) if slot == 0 else loc(p, 0, step)
-            start(source, origin, p, None, ring_send, ring_recv, ring_index(p, slot, kind), target)
+            start(source, origin, p, "all", ring_send, ring_recv, ring_index(p, slot, kind), target)
 
     def ring_pass(p, slot, kind, origin):
         step = 1 if kind == 0 else -1
@@ -147,15 +172,26 @@
         start(origin, origin, p, kind, ring_send, ring_recv, ring_index(p, slot, kind + 2), target)
 
     def ring_wait(p, slot, kind, origin):
-        half = kind - 2 if kind >= 2 else None
+        half = kind - 2 if kind >= 2 else "all"
         for copy in copies(origin, origin, p, half, ring_send, ring_recv, ring_index(p, slot, kind), partner):
             copy.wait_recv()
 
     def pair_index(p, first, second):
         return (p * 4 + OFFSETS.index(first)) * 4 + OFFSETS.index(second)
 
-    def pair_start(p, first, second, source, origin):
-        start(source, origin, p, None, pair_send, pair_recv, pair_index(p, first, second), partner)
+    def arrived(p, first, second, origin):
+        index = pair_index(p, first, second)
+        start(origin, origin, p, "all", pair_send, pair_recv, index, partner)
+        target = {"group": (group + (1 if p == 0 else groups - 1)) % groups}
+        start(origin, origin, p, "give", side_send, side_recv, index, target)
+
+    def side_wait(first, second):
+        for p in (0, 1):
+            origin = loc(p, first, second)
+            index = pair_index(p, first, second)
+            for copy in copies(origin, origin, p, "take", side_send, side_recv, index, partner):
+                copy.wait_recv()
+            start(origin, origin, p, "take", late_send, late_recv, index, partner)
 
     others = [(group + k) % groups for k in range(1, groups)]
     greet(
@@ -167,7 +203,7 @@
         ring_start(p, 0, None, dev)
     for p in (0, 1):
         ring_start(p, 1, None, dev)
-        pair_start(p, 0, 0, None, dev)
+        start(None, dev, p, "own", pair_send, pair_recv, pair_index(p, 0, 0), partner)
     own_rows = pl.ds(pl.multiple_of(group * rows, rows), rows)
     for k, other in enumerate(others):
         copy = remote(query, query_out.at[own_rows], query_send.at[k], query_recv.at[k], {"group": other})
@@ -188,26 +224,32 @@
             ring_wait(p, 0, kind, origin)
             ring_pass(p, 0, kind, origin)
             ring_start(p, slot, origin, origin)
-            pair_start(p, first, 0, origin, origin)
+            arrived(p, first, 0, origin)
     for p in (0, 1):
         origin = loc(p, 2, 0)
         ring_wait(p, 0, 2, origin)
         ring_wait(p, 0, 3, origin)
         ring_start(p, 4, origin, origin)
-        pair_start(p, 2, 0, origin, origin)
+        arrived(p, 2, 0, origin)
     for slot, first in ((1, 0), (2, -1), (3, 1), (4, 2)):
         for second, kind in ((-1, 0), (1, 1)):
             for p in (0, 1):
                 origin = loc(p, first, second)
                 ring_wait(p, slot, kind, origin)
                 ring_pass(p, slot, kind, origin)
-                pair_start(p, first, second, origin, origin)
+                arrived(p, first, second, origin)
+        if first != 0:
+            side_wait(first, 0)
     for slot, first in ((1, 0), (2, -1), (3, 1), (4, 2)):
         for p in (0, 1):
             origin = loc(p, first, 2)
             ring_wait(p, slot, 2, origin)
             ring_wait(p, slot, 3, origin)
-            pair_start(p, first, 2, origin, origin)
+            arrived(p, first, 2, origin)
+        side_wait(first, -1)
+        side_wait(first, 1)
+    for first in (0, -1, 1, 2):
+        side_wait(first, 2)
 
     for k in range(groups - 1):
         source = (group + groups - 1 - k) % groups
@@ -218,8 +260,13 @@
             for p in (0, 1):
                 origin = loc(p, first, second) + flip
                 index = pair_index(p, first, second)
-                for copy in copies(origin, origin, p, None, pair_send, pair_recv, index, partner):
+                own = first == 0 and second == 0
+                part = "own" if own else "all"
+                for copy in copies(origin, origin, p, part, pair_send, pair_recv, index, partner):
                     copy.wait_recv()
+                if not own:
+                    for copy in copies(origin, origin, p, "take", late_send, late_recv, index, partner):
+                        copy.wait_recv()
     for copy in kept:
         copy.wait()
 
@@ -281,6 +328,10 @@
             pltpu.VMEM(tokens.shape, jnp.float32),
             pltpu.SemaphoreType.DMA((40, 2)),
             pltpu.SemaphoreType.DMA((40, 2)),
+            pltpu.SemaphoreType.DMA((32, 2)),
+            pltpu.SemaphoreType.DMA((32, 2)),
+            pltpu.SemaphoreType.DMA((32, 2)),
+            pltpu.SemaphoreType.DMA((32, 2)),
             pltpu.SemaphoreType.DMA((32, 2)),
             pltpu.SemaphoreType.DMA((32, 2)),
             pltpu.SemaphoreType.DMA((groups - 1,)),

time: 105 us -> 104 us (level)
    pallas_call x1, Pallas kernels: 68 us -> 65 us  [encode(): pl.pallas_call(lambda *refs: weights_kernel(groups, *refs), out_shape=(ja...]
    pallas_call x1, Pallas kernels: 15.1 us -> 17.4 us  [gather_vectors(): pl.pallas_call(vectors_kernel, out_shape=jax.ShapeDtypeStruct((devs * row...]
where the time goes in v3:
time: 104 us
  Pallas kernels  100 us (96%)
  local copies, waits for them, and re-layouts  1.97 us (2%)
    pallas_call x1, Pallas kernels, encode(): pl.pallas_call(lambda *refs: weights_kernel(groups, *refs), out_shape=(ja...  65 us
    pallas_call x1, Pallas kernels, gather_vectors(): pl.pallas_call(vectors_kernel, out_shape=jax.ShapeDtypeStruct((devs * row...  17.4 us
    pallas_call x1, Pallas kernels, body(): pl.pallas_call(lambda *refs: score_kernel(query_len, *refs), out_shape=ja...  9.58 us
    pallas_call x1, Pallas kernels, pick_scores(): pl.pallas_call(lambda *refs: pick_kernel(groups, *refs), out_shape=jax.Sh...  8.28 us

profile of v3, /device:TPU:1, one launch (start us, length us, event | category | flops | bytes accessed | tf_op | source)
XLA Modules:
  0.0 103.6 jit_solution(1462360263941326485)
XLA Ops:
  0.6 65.0 %encode.1 = (bf16[512,128]{1,0:T(8,128)(2,1)}, bf16[128,128]{1,0:T(8,128)(2,1)}) custom-call(bf16[32,5248]{1,0:T(8,128)(2,1)} %refs_0_.1, bf16[82,1024]{1,0:T(8,128)(2,1)} %refs_1_.2, bf16[64,128]{1,0:T(8,128)(2,1)} %bitcast.4, bf16[128,1024]{1,0:T(8,128)(2,1)} %refs_3_.1, f32[1,1024]{1,0:T(1,128)} %bitcast.5, f32[1,1024]{1,0:T(1,128)} %bitcast.6, ...), custom_call_target="tpu_custom_call" | custom-call | tf_op jit(solution)/shard_map/encode/pallas_call | solution.py:314
  65.7 17.4 %vectors.1.refs_1_ = bf16[4096,128]{1,0:T(8,128)(2,1)} custom-call(bf16[128,128]{1,0:T(8,128)(2,1)} %get-tuple-element.8.vec), custom_call_target="tpu_custom_call" | custom-call | tf_op jit(solution)/shard_map/vectors/pallas_call | solution.py:379
  83.0 0.0 copy-start.2
  83.0 0.6 copy-done.2
  83.7 0.1 copy.12
  83.8 0.6 reduce.refs_0_
  84.4 0.0 copy-start
  84.4 9.6 %score.1.refs_0_ = f32[16,128]{1,0:T(8,128)} custom-call(s32[16]{0:T(128)} %reduce.refs_0_, bf16[4096,128]{1,0:T(8,128)(2,1)} %vectors.1.refs_1_, bf16[512,128]{1,0:T(8,128)(2,1)} %get-tuple-element.5.refs_2_), custom_call_target="tpu_custom_call" | custom-call | tf_op jit(solution)/shard_map/score/pallas_call | solution.py:472
  94.0 8.3 %pick.1 = f32[2,100]{1,0:T(2,128)} custom-call(f32[16,128]{1,0:T(8,128)} %score.1.refs_0_, s32[2,100]{1,0:T(2,128)} %refs_1_.3), custom_call_target="tpu_custom_call" | custom-call | tf_op jit(solution)/shard_map/pick/pallas_call | solution.py:428
  102.3 0.0 copy-done
  102.3 0.0 copy-start.1
  102.3 0.6 copy.15
  102.9 0.1 copy-done.1
  103.0 0.6 copy.16
  (1 shorter events, 0.0 us)
Async XLA Ops:
  83.0 0.7 copy-start.2
  84.4 17.9 %copy-start = (bf16[128,128]{1,0:T(8,128)(2,1)S(1)}, bf16[128,128]{1,0:T(8,128)(2,1)}, u32[]{:S(2)}) copy-start(bf16[128,128]{1,0:T(8,128)(2,1)} %get-tuple-element.8.vec) | copy-start | bytes 98308
  102.3 0.7 copy-start.1

commit v4 on v3

--- a/solution.py
+++ b/solution.py
@@ -19,7 +19,7 @@
     tokens = vec_ref.shape[0]
     blocks = tokens // BLOCK
     width = query_rows.shape[0]
-    row_ids = lax.broadcasted_iota(jnp.int32, (BLOCK, width), 0)
+    row_ids = lax.broadcasted_iota(jnp.int32, (BLOCK, 1), 0)
     doc_ids = lax.broadcasted_iota(jnp.int32, (doc_count, width), 0)
 
     def step(_, state):
@@ -35,14 +35,20 @@
             preferred_element_type=jnp.float32,
         )
         inside = (row_ids >= place - first) & (row_ids < stop - first)
-        top = jnp.max(jnp.where(inside, similar, -jnp.inf), axis=0, keepdims=True)
+        top = jnp.max(similar + jnp.where(inside, 0.0, -jnp.inf), axis=0, keepdims=True)
         best = jnp.where(doc_ids == doc, jnp.maximum(best, top), best)
         doc = jnp.minimum(doc + (stop == doc_end).astype(jnp.int32), doc_count - 1)
         return stop, doc, best
 
     start = jnp.full((doc_count, width), -jnp.inf, jnp.float32)
     state = (jnp.int32(0), jnp.int32(0), start)
-    return lax.fori_loop(0, blocks + doc_count - 1, step, state)[2]
+
+    def steps(i, state):
+        for _ in range(STEPS):
+            state = step(i, state)
+        return state
+
+    return lax.fori_loop(0, pl.cdiv(blocks + doc_count - 1, STEPS), steps, state)[2]
 
 
 def score_kernel(query_len, ends_ref, vec_ref, query_ref, out_ref):
@@ -58,6 +64,8 @@
 SIDE = 4
 OFFSETS = (0, -1, 1, 2)
 TILE = 512
+CROSS = (1, 2)
+STEPS = 4
 
 
 def place():
@@ -184,6 +192,9 @@
         start(origin, origin, p, "all", pair_send, pair_recv, index, partner)
         target = {"group": (group + (1 if p == 0 else groups - 1)) % groups}
         start(origin, origin, p, "give", side_send, side_recv, index, target)
+        if second in CROSS:
+            target = {"group": (group + (1 if p == 1 else groups - 1)) % groups, "dev": partner}
+            start(origin, origin, p, "give", late_send, late_recv, index, target)
 
     def side_wait(first, second):
         for p in (0, 1):
@@ -191,13 +202,15 @@
             index = pair_index(p, first, second)
             for copy in copies(origin, origin, p, "take", side_send, side_recv, index, partner):
                 copy.wait_recv()
-            start(origin, origin, p, "take", late_send, late_recv, index, partner)
+            if second not in CROSS:
+                start(origin, origin, p, "take", late_send, late_recv, index, partner)
 
     others = [(group + k) % groups for k in range(1, groups)]
     greet(
         [{"dev": at(*d)} for d in ((1, 0), (-1, 0), (0, 1), (0, -1))]
         + [{"dev": partner}]
         + [{"group": other} for other in others]
+        + [{"group": others[k], "dev": partner} for k in (0, -1)]
     )
     for p in (0, 1):
         ring_start(p, 0, None, dev)

time: 104 us -> 111 us (1.067)
  Pallas kernels: 100 us -> 107 us
    pallas_call x1, Pallas kernels: 65 us -> 75.8 us  [encode(): pl.pallas_call(lambda *refs: weights_kernel(groups, *refs), out_shape=(ja...]
    pallas_call x1, Pallas kernels: 9.58 us -> 5.6 us  [body(): pl.pallas_call(lambda *refs: score_kernel(query_len, *refs), out_shape=ja...]
where the time goes in v4:
time: 111 us; the launch traced here: 110 us
  Pallas kernels  107 us (96%)
  local copies, waits for them, and re-layouts  1.97 us (2%)
    pallas_call x1, Pallas kernels, encode(): pl.pallas_call(lambda *refs: weights_kernel(groups, *refs), out_shape=(ja...  75.8 us
    pallas_call x1, Pallas kernels, gather_vectors(): pl.pallas_call(vectors_kernel, out_shape=jax.ShapeDtypeStruct((devs * row...  17.5 us
    pallas_call x1, Pallas kernels, pick_scores(): pl.pallas_call(lambda *refs: pick_kernel(groups, *refs), out_shape=jax.Sh...  8.25 us
    pallas_call x1, Pallas kernels, body(): pl.pallas_call(lambda *refs: score_kernel(query_len, *refs), out_shape=ja...  5.6 us

profile of v4, /device:TPU:1, one launch (start us, length us, event | category | flops | bytes accessed | tf_op | source)
XLA Modules:
  0.0 110.4 jit_solution(12860997421585468538)
XLA Ops:
  0.6 75.8 %encode.1 = (bf16[512,128]{1,0:T(8,128)(2,1)}, bf16[128,128]{1,0:T(8,128)(2,1)}) custom-call(bf16[32,5248]{1,0:T(8,128)(2,1)} %refs_0_.1, bf16[82,1024]{1,0:T(8,128)(2,1)} %refs_1_.2, bf16[64,128]{1,0:T(8,128)(2,1)} %bitcast.4, bf16[128,1024]{1,0:T(8,128)(2,1)} %refs_3_.1, f32[1,1024]{1,0:T(1,128)} %bitcast.5, f32[1,1024]{1,0:T(1,128)} %bitcast.6, ...), custom_call_target="tpu_custom_call" | custom-call | tf_op jit(solution)/shard_map/encode/pallas_call | solution.py:327
  76.4 17.5 %vectors.1.refs_1_ = bf16[4096,128]{1,0:T(8,128)(2,1)} custom-call(bf16[128,128]{1,0:T(8,128)(2,1)} %get-tuple-element.8.vec), custom_call_target="tpu_custom_call" | custom-call | tf_op jit(solution)/shard_map/vectors/pallas_call | solution.py:392
  93.9 0.0 copy-start.2
  93.9 0.6 copy-done.2
  94.6 0.1 copy.12
  94.7 0.6 reduce.refs_0_
  95.3 0.0 copy-start
  95.3 5.6 %score.1.refs_0_ = f32[16,128]{1,0:T(8,128)} custom-call(s32[16]{0:T(128)} %reduce.refs_0_, bf16[4096,128]{1,0:T(8,128)(2,1)} %vectors.1.refs_1_, bf16[512,128]{1,0:T(8,128)(2,1)} %get-tuple-element.5.refs_2_), custom_call_target="tpu_custom_call" | custom-call | tf_op jit(solution)/shard_map/score/pallas_call | solution.py:485
  100.9 8.3 %pick.1 = f32[2,100]{1,0:T(2,128)} custom-call(f32[16,128]{1,0:T(8,128)} %score.1.refs_0_, s32[2,100]{1,0:T(2,128)} %refs_1_.3), custom_call_target="tpu_custom_call" | custom-call | tf_op jit(solution)/shard_map/pick/pallas_call | solution.py:441
  109.2 0.0 copy-done
  109.2 0.0 copy-start.1
  109.2 0.6 copy.15
  109.8 0.1 copy-done.1
  109.9 0.6 copy.16
  (1 shorter events, 0.0 us)
Async XLA Ops:
  93.9 0.7 copy-start.2
  95.3 13.9 %copy-start = (bf16[128,128]{1,0:T(8,128)(2,1)S(1)}, bf16[128,128]{1,0:T(8,128)(2,1)}, u32[]{:S(2)}) copy-start(bf16[128,128]{1,0:T(8,128)(2,1)} %get-tuple-element.8.vec) | copy-start | bytes 98308
  109.2 0.7 copy-start.1

commit v5 on v2

--- a/solution.py
+++ b/solution.py
@@ -19,7 +19,7 @@
     tokens = vec_ref.shape[0]
     blocks = tokens // BLOCK
     width = query_rows.shape[0]
-    row_ids = lax.broadcasted_iota(jnp.int32, (BLOCK, width), 0)
+    row_ids = lax.broadcasted_iota(jnp.int32, (BLOCK, 1), 0)
     doc_ids = lax.broadcasted_iota(jnp.int32, (doc_count, width), 0)
 
     def step(_, state):
@@ -35,14 +35,20 @@
             preferred_element_type=jnp.float32,
         )
         inside = (row_ids >= place - first) & (row_ids < stop - first)
-        top = jnp.max(jnp.where(inside, similar, -jnp.inf), axis=0, keepdims=True)
+        top = jnp.max(similar + jnp.where(inside, 0.0, -jnp.inf), axis=0, keepdims=True)
         best = jnp.where(doc_ids == doc, jnp.maximum(best, top), best)
         doc = jnp.minimum(doc + (stop == doc_end).astype(jnp.int32), doc_count - 1)
         return stop, doc, best
 
     start = jnp.full((doc_count, width), -jnp.inf, jnp.float32)
     state = (jnp.int32(0), jnp.int32(0), start)
-    return lax.fori_loop(0, blocks + doc_count - 1, step, state)[2]
+
+    def steps(i, state):
+        for _ in range(STEPS):
+            state = step(i, state)
+        return state
+
+    return lax.fori_loop(0, pl.cdiv(blocks + doc_count - 1, STEPS), steps, state)[2]
 
 
 def score_kernel(query_len, ends_ref, vec_ref, query_ref, out_ref):
@@ -58,6 +64,7 @@
 SIDE = 4
 OFFSETS = (0, -1, 1, 2)
 TILE = 512
+STEPS = 4
 
 
 def place():

time: 105 us -> 101 us (0.962)
  Pallas kernels: 101 us -> 97.3 us
    pallas_call x1, Pallas kernels: 9.57 us -> 5.6 us  [body(): pl.pallas_call(lambda *refs: score_kernel(query_len, *refs), out_shape=ja...]
where the time goes in v5:
time: 101 us
  Pallas kernels  97.3 us (96%)
  local copies, waits for them, and re-layouts  1.97 us (2%)
    pallas_call x1, Pallas kernels, encode(): pl.pallas_call(lambda *refs: weights_kernel(groups, *refs), out_shape=(ja...  68 us
    pallas_call x1, Pallas kernels, gather_vectors(): pl.pallas_call(vectors_kernel, out_shape=jax.ShapeDtypeStruct((devs * row...  15.1 us
    pallas_call x1, Pallas kernels, pick_scores(): pl.pallas_call(lambda *refs: pick_kernel(groups, *refs), out_shape=jax.Sh...  8.59 us
    pallas_call x1, Pallas kernels, body(): pl.pallas_call(lambda *refs: score_kernel(query_len, *refs), out_shape=ja...  5.6 us

profile of v5, /device:TPU:1, one launch (start us, length us, event | category | flops | bytes accessed | tf_op | source)
XLA Modules:
  0.0 100.6 jit_solution(6196620311742909892)
XLA Ops:
  0.6 68.0 %encode.1 = (bf16[512,128]{1,0:T(8,128)(2,1)}, bf16[128,128]{1,0:T(8,128)(2,1)}) custom-call(bf16[32,5248]{1,0:T(8,128)(2,1)} %refs_0_.1, bf16[82,1024]{1,0:T(8,128)(2,1)} %refs_1_.2, bf16[64,128]{1,0:T(8,128)(2,1)} %bitcast.4, bf16[128,1024]{1,0:T(8,128)(2,1)} %refs_3_.1, f32[1,1024]{1,0:T(1,128)} %bitcast.5, f32[1,1024]{1,0:T(1,128)} %bitcast.6, ...), custom_call_target="tpu_custom_call" | custom-call | tf_op jit(solution)/shard_map/encode/pallas_call | solution.py:274
  68.6 15.1 %vectors.1.refs_1_ = bf16[4096,128]{1,0:T(8,128)(2,1)} custom-call(bf16[128,128]{1,0:T(8,128)(2,1)} %get-tuple-element.8.vec), custom_call_target="tpu_custom_call" | custom-call | tf_op jit(solution)/shard_map/vectors/pallas_call | solution.py:335
  83.8 0.0 copy-start.2
  83.8 0.6 copy-done.2
  84.4 0.1 copy.12
  84.5 0.6 reduce.refs_0_
  85.2 0.0 copy-start
  85.2 5.6 %score.1.refs_0_ = f32[16,128]{1,0:T(8,128)} custom-call(s32[16]{0:T(128)} %reduce.refs_0_, bf16[4096,128]{1,0:T(8,128)(2,1)} %vectors.1.refs_1_, bf16[512,128]{1,0:T(8,128)(2,1)} %get-tuple-element.5.refs_2_), custom_call_target="tpu_custom_call" | custom-call | tf_op jit(solution)/shard_map/score/pallas_call | solution.py:428
  90.8 8.6 %pick.1 = f32[2,100]{1,0:T(2,128)} custom-call(f32[16,128]{1,0:T(8,128)} %score.1.refs_0_, s32[2,100]{1,0:T(2,128)} %refs_1_.3), custom_call_target="tpu_custom_call" | custom-call | tf_op jit(solution)/shard_map/pick/pallas_call | solution.py:384
  99.4 0.0 copy-done
  99.4 0.0 copy-start.1
  99.4 0.6 copy.15
  100.0 0.1 copy-done.1
  100.1 0.6 copy.16
  (1 shorter events, 0.0 us)
Async XLA Ops:
  83.8 0.7 copy-start.2
  85.2 14.2 %copy-start = (bf16[128,128]{1,0:T(8,128)(2,1)S(1)}, bf16[128,128]{1,0:T(8,128)(2,1)}, u32[]{:S(2)}) copy-start(bf16[128,128]{1,0:T(8,128)(2,1)} %get-tuple-element.8.vec) | copy-start | bytes 98308
  99.4 0.7 copy-start.1
